TPU v7x, 256 devices: a whole 4x4x8 slice. The times are simulated.
256 devices in a mesh: seq: 16 (over y_lo, x, core), tp: 16 (over z, y_hi).
Axes of the slice: x: 4, y: 4 (y_hi: 2, y_lo: 2; y = y_hi * 2 + y_lo), z: 8, core: 2. Of those that a mesh axis runs over, the one named last changes fastest.
Arguments:
- tokens: bfloat16 [4096, 5376], P('seq', 'tp'), may hold values from -24 to 24
- w_query: bfloat16 [5376, 4096], P('seq', 'tp'), may hold values from -0.078125 to 0.078125
- w_key: bfloat16 [5376, 2048], P('seq', 'tp'), may hold values from -0.078125 to 0.078125
- w_value: bfloat16 [5376, 2048], P('seq', 'tp'), may hold values from -0.078125 to 0.078125
- w_out: bfloat16 [4096, 5376], P('tp', 'seq'), may hold values from -0.09375 to 0.09375
- cotangent: bfloat16 [4096, 5376], P('seq', 'tp'), may hold values from -6 to 6
- block_lists: int32 [32, 9], P('seq'), may hold values from -1 to 31, as said below
Outputs:
- grad_tokens: bfloat16 [4096, 5376], P('seq', 'tp')
- grad_query: bfloat16 [5376, 4096], P('seq', 'tp')
- grad_key: bfloat16 [5376, 2048], P('seq', 'tp')
- grad_value: bfloat16 [5376, 2048], P('seq', 'tp')
- grad_w_out: bfloat16 [4096, 5376], P('tp', 'seq')
Inputs may be any that keep to these rules, and one draw needn't show every extreme that they name: `block_lists`: entry k of query block b is b - 8 + k if that key block lies in the same document as block b, else -1. Documents are runs of whole blocks; the last entry of each row is b, and the valid entries of a row are its last ones.
All inputs are finite; a program needn't handle non-finite values.
Results may differ from a plain program's by a relative error of at most 0.025.
Values may be sent and summed in bfloat16 or wider, within the bound.
No kernel may reach another device: no remote copies, remote signals or barrier semaphores. Data moves between devices by JAX's collectives and lax.ppermute only.
A program may use at most 64 MiB of HBM per device.

v0:
```python
import jax
import jax.numpy as jnp
from jax import lax
from jax.sharding import PartitionSpec as P

HEADS = 32
KV_HEADS = 16
HD = 128
WIN = 1024
ATTN_SCALAR = 168


def from_behind(block, axis, distance):
    devices = range(lax.axis_size(axis))
    route = [(i - distance, i) for i in devices if i - distance in devices]
    return lax.ppermute(block, axis, route)


def window_view(blocks, n_blocks, span):
    return jnp.concatenate([blocks[offset : offset + n_blocks] for offset in range(span)], axis=1)


def fold_windows(windows, n_blocks, span, block_len):
    shaped = windows.reshape(n_blocks, span, block_len, windows.shape[2], windows.shape[3])
    summed = jnp.zeros(
        (n_blocks + span - 1, block_len, windows.shape[2], windows.shape[3]), jnp.float32
    )
    for offset in range(span):
        summed = summed.at[offset : offset + n_blocks].add(shaped[:, offset])
    return summed.reshape((n_blocks + span - 1) * block_len, windows.shape[2] * windows.shape[3])


def local_attention(query, keys, values, d_attn, block_lists, softmax_scale):
    tok_rows, kv_local, group_size, head_dim = query.shape
    n_blocks, span = block_lists.shape
    block_len = tok_rows // n_blocks
    width = span * block_len
    key_blocks = keys.reshape(n_blocks + span - 1, block_len, kv_local, head_dim)
    val_blocks = values.reshape(n_blocks + span - 1, block_len, kv_local, head_dim)
    key_win = window_view(key_blocks, n_blocks, span)
    val_win = window_view(val_blocks, n_blocks, span)
    q_blocks = query.reshape(n_blocks, block_len, kv_local, group_size, head_dim)
    grad_blocks = d_attn.reshape(n_blocks, block_len, kv_local, group_size, head_dim)
    scores = (
        jnp.einsum("btkgd,bwkd->bkgtw", q_blocks, key_win, preferred_element_type=jnp.float32)
        * softmax_scale
    )
    rows_at = jnp.arange(block_len)[:, None]
    cols_at = jnp.arange(width)[None, :]
    inside = (cols_at > rows_at) & (cols_at <= rows_at + (width - block_len))
    listed = jnp.repeat(block_lists >= 0, block_len, axis=1)
    allowed = inside[None, None, None] & listed[:, None, None, None, :]
    masked = jnp.where(allowed, scores, -1e30)
    highest = jnp.max(masked, axis=-1, keepdims=True)
    weights = jnp.where(allowed, jnp.exp(masked - highest), 0.0)
    probs = weights / jnp.sum(weights, axis=-1, keepdims=True)
    probs_half = probs.astype(jnp.bfloat16)
    attn = jnp.einsum(
        "bkgtw,bwkd->btkgd", probs_half, val_win, preferred_element_type=jnp.float32
    ).astype(jnp.bfloat16)
    delta = jnp.sum(grad_blocks.astype(jnp.float32) * attn.astype(jnp.float32), axis=-1)
    delta = jnp.transpose(delta, (0, 2, 3, 1))[..., None]
    grad_probs = jnp.einsum(
        "btkgd,bwkd->bkgtw", grad_blocks, val_win, preferred_element_type=jnp.float32
    )
    grad_scores = (probs * (grad_probs - delta)).astype(jnp.bfloat16)
    grad_q = (
        jnp.einsum("bkgtw,bwkd->btkgd", grad_scores, key_win, preferred_element_type=jnp.float32)
        * softmax_scale
    ).astype(jnp.bfloat16)
    grad_kwin = (
        jnp.einsum("bkgtw,btkgd->bwkd", grad_scores, q_blocks, preferred_element_type=jnp.float32)
        * softmax_scale
    )
    grad_vwin = jnp.einsum(
        "bkgtw,btkgd->bwkd", probs_half, grad_blocks, preferred_element_type=jnp.float32
    )
    grad_keys = fold_windows(grad_kwin, n_blocks, span, block_len)
    grad_values = fold_windows(grad_vwin, n_blocks, span, block_len)
    flat = kv_local * group_size * head_dim
    return (attn.reshape(tok_rows, flat), grad_q.reshape(tok_rows, flat), grad_keys, grad_values)


def contract_cols(left, right):
    return lax.dot_general(
        left, right, (((1,), (1,)), ((), ())), preferred_element_type=jnp.float32
    )


def term_maker(left, right):
    return lax.dot_general(
        left, right, (((0,), (0,)), ((), ())), preferred_element_type=jnp.float32
    )


def shards(tokens, w_query, w_key, w_value, w_out, cotangent, block_lists):
    softmax_scale = ATTN_SCALAR ** (-0.5)
    group_size = HEADS // KV_HEADS
    head_dim = HD
    tok_rows = tokens.shape[0]
    reach = WIN // tok_rows
    full_tokens, full_cot = (
        lax.all_gather(tokens, "tp", axis=1, tiled=True),
        lax.all_gather(cotangent, "tp", axis=1, tiled=True),
    )
    query_full, key_full, value_full = (
        lax.all_gather(w_query, "seq", axis=0, tiled=True),
        lax.all_gather(w_key, "seq", axis=0, tiled=True),
        lax.all_gather(w_value, "seq", axis=0, tiled=True),
    )
    d_attn = contract_cols(full_cot, lax.all_gather(w_out, "seq", axis=1, tiled=True)).astype(
        jnp.bfloat16
    )
    query = jnp.dot(full_tokens, query_full, preferred_element_type=jnp.float32).astype(
        jnp.bfloat16
    )
    keys = jnp.dot(full_tokens, key_full, preferred_element_type=jnp.float32).astype(jnp.bfloat16)
    values = jnp.dot(full_tokens, value_full, preferred_element_type=jnp.float32).astype(
        jnp.bfloat16
    )
    earlier = [from_behind((keys, values), "seq", distance) for distance in range(reach, 0, -1)]
    key_ext = jnp.concatenate([member[0] for member in earlier] + [keys], axis=0)
    value_ext = jnp.concatenate([member[1] for member in earlier] + [values], axis=0)
    kv_local = keys.shape[1] // head_dim
    attn, grad_q, grad_k_ext, grad_v_ext = local_attention(
        query.reshape(tok_rows, kv_local, group_size, head_dim),
        key_ext.reshape(-1, kv_local, head_dim),
        value_ext.reshape(-1, kv_local, head_dim),
        d_attn.reshape(tok_rows, kv_local, group_size, head_dim),
        block_lists,
        softmax_scale,
    )

    def segment(array, index):
        return array[index * tok_rows : (index + 1) * tok_rows]

    summed_k = segment(grad_k_ext, reach)
    summed_v = segment(grad_v_ext, reach)
    for distance in range(1, reach + 1):
        back_k, back_v = from_behind(
            (segment(grad_k_ext, reach - distance), segment(grad_v_ext, reach - distance)),
            "seq",
            -distance,
        )
        summed_k = summed_k + back_k
        summed_v = summed_v + back_v
    grad_k = summed_k.astype(jnp.bfloat16)
    grad_v = summed_v.astype(jnp.bfloat16)
    token_term = (
        contract_cols(grad_q, query_full)
        + contract_cols(grad_k, key_full)
        + contract_cols(grad_v, value_full)
    )
    grad_tokens = lax.psum_scatter(token_term, "tp", scatter_dimension=1, tiled=True).astype(
        jnp.bfloat16
    )
    operand_pairs = (
        (full_tokens, grad_q),
        (full_tokens, grad_k),
        (full_tokens, grad_v),
        (full_cot, attn),
    )

    def reduce_rows(left, right):
        return lax.psum_scatter(
            term_maker(left, right).astype(jnp.bfloat16), "seq", scatter_dimension=0, tiled=True
        ).astype(jnp.float32)

    results = [reduce_rows(left, right) for left, right in operand_pairs]
    grad_query = results[0].astype(jnp.bfloat16)
    grad_key = results[1].astype(jnp.bfloat16)
    grad_value = results[2].astype(jnp.bfloat16)
    grad_w_out = results[3].T.astype(jnp.bfloat16)
    return (grad_tokens, grad_query, grad_key, grad_value, grad_w_out)


def solution(mesh):
    in_specs = (
        P("seq", "tp"),
        P("seq", "tp"),
        P("seq", "tp"),
        P("seq", "tp"),
        P("tp", "seq"),
        P("seq", "tp"),
        P("seq", None),
    )
    out_specs = (P("seq", "tp"), P("seq", "tp"), P("seq", "tp"), P("seq", "tp"), P("tp", "seq"))
    return jax.shard_map(shards, mesh=mesh, in_specs=in_specs, out_specs=out_specs, check_vma=False)
```

profile of v0, /device:TPU:32, one launch (start us, length us, event | category | flops | bytes accessed | tf_op | source)
XLA Modules:
  0.0 933.3 jit_solution(3593583309488818795)
XLA Ops:
  12.6 35.0 %all-gather.9.cloned.1.call-done = bf16[5376,128]{1,0:T(8,128)(2,1)} async-done(((bf16[336,128]{1,0:T(8,128)(2,1)}), bf16[5376,128]{1,0:T(8,128)(2,1)}) %all-gather.9.cloned.1.call-update) | async-done | bytes 1376272 | tf_op jit(solution)/shard_map/all_gather | solution.py:108
  47.6 92.1 %all-gather.7.cloned.1.call-done = bf16[256,5376]{0,1:T(8,128)(2,1)} async-done(((bf16[256,336]{0,1:T(8,128)(2,1)}), bf16[256,5376]{0,1:T(8,128)(2,1)}) %all-gather.7.cloned.1.call-update) | async-done | bytes 2752528 | tf_op jit(solution)/shard_map/all_gather | solution.py:103
  139.7 3.2 convolution_convert_fusion.7
  143.0 5.5 collective-permute-start
  148.5 1.9 collective-permute-start.1
  150.4 3.1 collective-permute-start.2
  153.4 3.3 collective-permute-start.3
  156.7 20.5 %all-gather.11.cloned.1.call-done = bf16[5376,256]{1,0:T(8,128)(2,1)} async-done(((bf16[336,256]{1,0:T(8,128)(2,1)}), bf16[5376,256]{1,0:T(8,128)(2,1)}) %all-gather.11.cloned.1.call-update) | async-done | bytes 2752528 | tf_op jit(solution)/shard_map/all_gather | solution.py:107
  177.2 3.4 convolution_convert_fusion.5
  180.6 87.6 %all-gather.15.cloned.1.call-done = bf16[256,5376]{0,1:T(8,128)(2,1)} async-done(((bf16[256,336]{0,1:T(8,128)(2,1)}), bf16[256,5376]{0,1:T(8,128)(2,1)}) %all-gather.15.cloned.1.call-update) | async-done | bytes 2752528 | tf_op jit(solution)/shard_map/all_gather | solution.py:104
  268.2 36.3 %all-gather.17.cloned.1.call-done = bf16[256,5376]{0,1:T(8,128)(2,1)} async-done(((bf16[256,336]{0,1:T(8,128)(2,1)}), bf16[256,5376]{0,1:T(8,128)(2,1)}) %all-gather.17.cloned.1.call-update) | async-done | bytes 2752528 | tf_op jit(solution)/shard_map/all_gather | solution.py:111
  304.5 3.5 convolution_convert_fusion.4
  308.0 33.5 %all-gather.13.cloned.1.call-done = bf16[5376,128]{1,0:T(8,128)(2,1)} async-done(((bf16[336,128]{1,0:T(8,128)(2,1)}), bf16[5376,128]{1,0:T(8,128)(2,1)}) %all-gather.13.cloned.1.call-update) | async-done | bytes 1376272 | tf_op jit(solution)/shard_map/all_gather | solution.py:109
  341.5 2.3 convolution_convert_fusion.6
  344.5 1.0 reshape.830
  345.5 1.6 reshape.805
  347.1 1.7 copy.86
  348.8 1.7 copy.97
  350.5 4.0 collective-permute-start.4
  355.3 2.0 collective-permute-start.5
  358.2 3.5 collective-permute-start.6
  361.6 3.0 collective-permute-start.7
  368.2 1.4 fusion.79
  370.1 1.8 convolution_bitcast_fusion.1
  373.8 1.5 fusion.11
  375.7 2.7 copy.99
  380.3 0.9 fusion.53
  381.3 0.9 fusion.51
  382.2 0.9 fusion.49
  383.2 0.9 fusion.47
  384.1 0.9 fusion.45
  386.0 1.7 fusion.41
  387.7 1.3 collective-permute-start.12
  389.0 2.7 copy.88
  396.4 0.9 fusion.60
  399.3 1.7 fusion.54
  401.0 1.3 collective-permute-start.10
  402.3 1.3 collective-permute-start.11
  403.6 1.3 collective-permute-start.8
  404.9 1.5 collective-permute-start.9
  406.5 2.8 fusion.39
  409.4 1.3 collective-permute-start.13
  410.7 2.9 collective-permute-done.11
  413.6 1.3 collective-permute-start.14
  414.9 1.3 collective-permute-start.15
  416.2 1.1 fusion.74
  418.3 1.4 collective-permute-done.13
  419.6 1.4 collective-permute-done.14
  421.0 5.3 collective-permute-done.15
  426.4 3.3 convolution_add_fusion
  429.7 2.2 fusion.3
  431.9 2.5 copy.131
  434.5 2.2 fusion.2
  436.7 2.5 copy.129
  439.2 2.6 fusion
  441.8 4.5 copy.127
  446.6 2.8 fusion.1
  449.4 2.9 copy.133
  452.3 201.1 %reduce-scatter.14.cloned.1.call-done = f32[256,336]{0,1:T(8,128)} async-done(((f32[256,5376]{0,1:T(8,128)}), f32[256,336]{0,1:T(8,128)}) %reduce-scatter.14.cloned.1.call-update) | async-done | bytes 344080 | tf_op jit(solution)/shard_map/reduce_scatter | solution.py:154
  653.4 1.7 convert_element_type.114
  655.1 65.9 %reduce-scatter.20.cloned.1.call-done = bf16[336,128]{1,0:T(8,128)(2,1)} async-done(((bf16[5376,128]{1,0:T(8,128)(2,1)}), bf16[336,128]{1,0:T(8,128)(2,1)}) %reduce-scatter.20.cloned.1.call-update) | async-done | bytes 86032
  721.0 67.3 %reduce-scatter.18.cloned.1.call-done = bf16[336,128]{1,0:T(8,128)(2,1)} async-done(((bf16[5376,128]{1,0:T(8,128)(2,1)}), bf16[336,128]{1,0:T(8,128)(2,1)}) %reduce-scatter.18.cloned.1.call-update) | async-done | bytes 86032
  788.2 69.2 %reduce-scatter.16.cloned.1.call-done = bf16[336,256]{1,0:T(8,128)(2,1)} async-done(((bf16[5376,256]{1,0:T(8,128)(2,1)}), bf16[336,256]{1,0:T(8,128)(2,1)}) %reduce-scatter.16.cloned.1.call-update) | async-done | bytes 172048
  857.4 69.3 %reduce-scatter.22.cloned.1.call-done = bf16[336,256]{1,0:T(8,128)(2,1)} async-done(((bf16[5376,256]{1,0:T(8,128)(2,1)}), bf16[336,256]{1,0:T(8,128)(2,1)}) %reduce-scatter.22.cloned.1.call-update) | async-done | bytes 172048
  (102 shorter events, 24.8 us)
Async XLA Ops:
  7.2 40.4 %all-gather.9.cloned.1.call-start = ((), (), s32[]{:S(2)}) async-start(), calls=%async_computation.6 | async-start | bytes 1462272 | tf_op jit(solution)/shard_map/all_gather | solution.py:108
  7.9 131.8 %all-gather.7.cloned.1.call-start = ((), (), s32[]{:S(2)}) async-start(), calls=%async_computation.5 | async-start | bytes 2924544 | tf_op jit(solution)/shard_map/all_gather | solution.py:103
  8.6 168.6 %all-gather.11.cloned.1.call-start = ((), (), s32[]{:S(2)}) async-start(), calls=%async_computation.7 | async-start | bytes 2924544 | tf_op jit(solution)/shard_map/all_gather | solution.py:107
  9.4 258.8 %all-gather.15.cloned.1.call-start = ((), (), s32[]{:S(2)}) async-start(), calls=%async_computation.9 | async-start | bytes 2924544 | tf_op jit(solution)/shard_map/all_gather | solution.py:104
  10.0 294.5 %all-gather.17.cloned.1.call-start = ((), (), s32[]{:S(2)}) async-start(), calls=%async_computation.10 | async-start | bytes 2924544 | tf_op jit(solution)/shard_map/all_gather | solution.py:111
  10.5 331.0 %all-gather.13.cloned.1.call-start = ((), (), s32[]{:S(2)}) async-start(), calls=%async_computation.8 | async-start | bytes 1462272 | tf_op jit(solution)/shard_map/all_gather | solution.py:109
  11.1 642.3 %reduce-scatter.14.cloned.1.call-start = ((), (), s32[]{:S(2)}) async-start(), calls=%async_computation.11 | async-start | bytes 5849088 | tf_op jit(solution)/shard_map/reduce_scatter | solution.py:154
  139.7 37.5 %copy-start = (bf16[256,5376]{0,1:T(8,128)(2,1)S(1)}, bf16[256,5376]{0,1:T(8,128)(2,1)}, u32[]{:S(2)}) copy-start(bf16[256,5376]{0,1:T(8,128)(2,1)} %all-gather.7.cloned.1.call-done) | copy-start | bytes 8257540
  143.0 212.3 %collective-permute-start = (bf16[256,128]{1,0:T(8,128)(2,1)S(1)}, bf16[256,128]{1,0:T(8,128)(2,1)}, u32[]{:S(2)}, u32[]{:S(2)}) collective-permute-start(bf16[256,128]{1,0:T(8,128)(2,1)S(1)} %convolution_convert_fusion.7), channel_id=1, source_target_pairs={{0,64},{16,80},{32,96},{48,112},{64,128},{80,144},{96,160},{112,17... | collective-permute-start | bytes 196616 | tf_op jit(solution)/shard_map/ppermute | solution.py:16
  148.5 209.7 %collective-permute-start.1 = (bf16[256,128]{1,0:T(8,128)(2,1)S(1)}, bf16[256,128]{1,0:T(8,128)(2,1)}, u32[]{:S(2)}, u32[]{:S(2)}) collective-permute-start(bf16[256,128]{1,0:T(8,128)(2,1)S(1)} %convolution_convert_fusion.7), channel_id=1, source_target_pairs={{0,48},{16,64},{32,80},{48,96},{64,112},{80,128},{96,144},{112,160... | collective-permute-start | bytes 196616 | tf_op jit(solution)/shard_map/ppermute | solution.py:16
  150.4 211.3 %collective-permute-start.2 = (bf16[256,128]{1,0:T(8,128)(2,1)S(1)}, bf16[256,128]{1,0:T(8,128)(2,1)}, u32[]{:S(2)}, u32[]{:S(2)}) collective-permute-start(bf16[256,128]{1,0:T(8,128)(2,1)S(1)} %convolution_convert_fusion.7), channel_id=1, source_target_pairs={{0,32},{16,48},{32,64},{48,80},{64,96},{80,112},{96,128},{112,144}... | collective-permute-start | bytes 196616 | tf_op jit(solution)/shard_map/ppermute | solution.py:16
  153.4 211.2 %collective-permute-start.3 = (bf16[256,128]{1,0:T(8,128)(2,1)S(1)}, bf16[256,128]{1,0:T(8,128)(2,1)}, u32[]{:S(2)}, u32[]{:S(2)}) collective-permute-start(bf16[256,128]{1,0:T(8,128)(2,1)S(1)} %convolution_convert_fusion.7), channel_id=1, source_target_pairs={{0,16},{16,32},{32,48},{48,64},{64,80},{80,96},{96,112},{112,128},... | collective-permute-start | bytes 196616 | tf_op jit(solution)/shard_map/ppermute | solution.py:16
  308.0 35.8 %copy-start.4 = (bf16[256,256]{1,0:T(8,128)(2,1)}, bf16[256,256]{1,0:T(8,128)(2,1)S(1)}, u32[]{:S(2)}) copy-start(bf16[256,256]{1,0:T(8,128)(2,1)S(1)} %convolution_convert_fusion.4) | copy-start | bytes 393220
  350.5 21.4 %collective-permute-start.4 = (bf16[256,128]{1,0:T(8,128)(2,1)S(1)}, bf16[256,128]{1,0:T(8,128)(2,1)S(1)}, u32[]{:S(2)}, u32[]{:S(2)}) collective-permute-start(bf16[256,128]{1,0:T(8,128)(2,1)S(1)} %convolution_convert_fusion.6), channel_id=1, source_target_pairs={{0,64},{16,80},{32,96},{48,112},{64,128},{80,144},{96,160},{112,17... | collective-permute-start | bytes 196616 | tf_op jit(solution)/shard_map/ppermute | solution.py:16
  355.3 16.6 %collective-permute-start.5 = (bf16[256,128]{1,0:T(8,128)(2,1)S(1)}, bf16[256,128]{1,0:T(8,128)(2,1)S(1)}, u32[]{:S(2)}, u32[]{:S(2)}) collective-permute-start(bf16[256,128]{1,0:T(8,128)(2,1)S(1)} %convolution_convert_fusion.6), channel_id=1, source_target_pairs={{0,48},{16,64},{32,80},{48,96},{64,112},{80,128},{96,144},{112,160... | collective-permute-start | bytes 196616 | tf_op jit(solution)/shard_map/ppermute | solution.py:16
  358.2 13.8 %collective-permute-start.6 = (bf16[256,128]{1,0:T(8,128)(2,1)S(1)}, bf16[256,128]{1,0:T(8,128)(2,1)S(1)}, u32[]{:S(2)}, u32[]{:S(2)}) collective-permute-start(bf16[256,128]{1,0:T(8,128)(2,1)S(1)} %convolution_convert_fusion.6), channel_id=1, source_target_pairs={{0,32},{16,48},{32,64},{48,80},{64,96},{80,112},{96,128},{112,144}... | collective-permute-start | bytes 196616 | tf_op jit(solution)/shard_map/ppermute | solution.py:16
  361.6 10.3 %collective-permute-start.7 = (bf16[256,128]{1,0:T(8,128)(2,1)S(1)}, bf16[256,128]{1,0:T(8,128)(2,1)S(1)}, u32[]{:S(2)}, u32[]{:S(2)}) collective-permute-start(bf16[256,128]{1,0:T(8,128)(2,1)S(1)} %convolution_convert_fusion.6), channel_id=1, source_target_pairs={{0,16},{16,32},{32,48},{48,64},{64,80},{80,96},{96,112},{112,128},... | collective-permute-start | bytes 196616 | tf_op jit(solution)/shard_map/ppermute | solution.py:16
  368.2 1.9 copy-start.6
  370.1 2.0 copy-start.5
  372.9 0.9 copy-start.3
  387.7 30.5 %collective-permute-start.12 = (f32[256,128]{1,0:T(8,128)}, f32[256,128]{1,0:T(8,128)S(1)}, u32[]{:S(2)}, u32[]{:S(2)}) collective-permute-start(f32[256,128]{1,0:T(8,128)} %bitcast.73), channel_id=1, source_target_pairs={{16,0},{32,16},{48,32},{64,48},{80,64},{96,80},{112,96},{128,112},... | collective-permute-start | bytes 393224 | tf_op jit(solution)/shard_map/ppermute | solution.py:16
  401.0 8.4 collective-permute-start.10
  402.3 11.3 %collective-permute-start.11 = (f32[256,128]{1,0:T(8,128)}, f32[256,128]{1,0:T(8,128)}, u32[]{:S(2)}, u32[]{:S(2)}) collective-permute-start(f32[256,128]{1,0:T(8,128)} %bitcast.57), channel_id=1, source_target_pairs={{64,0},{80,16},{96,32},{112,48},{128,64},{144,80},{160,96},{176,11... | collective-permute-start | bytes 393224 | tf_op jit(solution)/shard_map/ppermute | solution.py:16
  403.6 11.3 %collective-permute-start.8 = (f32[256,128]{1,0:T(8,128)}, f32[256,128]{1,0:T(8,128)}, u32[]{:S(2)}, u32[]{:S(2)}) collective-permute-start(f32[256,128]{1,0:T(8,128)} %bitcast.54), channel_id=1, source_target_pairs={{16,0},{32,16},{48,32},{64,48},{80,64},{96,80},{112,96},{128,112},... | collective-permute-start | bytes 393224 | tf_op jit(solution)/shard_map/ppermute | solution.py:16
  404.9 11.3 %collective-permute-start.9 = (f32[256,128]{1,0:T(8,128)}, f32[256,128]{1,0:T(8,128)}, u32[]{:S(2)}, u32[]{:S(2)}) collective-permute-start(f32[256,128]{1,0:T(8,128)} %bitcast.55), channel_id=1, source_target_pairs={{32,0},{48,16},{64,32},{80,48},{96,64},{112,80},{128,96},{144,112}... | collective-permute-start | bytes 393224 | tf_op jit(solution)/shard_map/ppermute | solution.py:16
  406.5 2.9 copy-start.9
  406.5 7.1 copy-start.8
  406.5 8.4 copy-start.7
  406.5 10.8 %copy-start.1 = (bf16[5376,128]{1,0:T(8,128)(2,1)S(1)}, bf16[5376,128]{1,0:T(8,128)(2,1)}, u32[]{:S(2)}) copy-start(bf16[5376,128]{1,0:T(8,128)(2,1)} %all-gather.9.cloned.1.call-done) | copy-start | bytes 4128772
  409.4 10.3 %collective-permute-start.13 = (f32[256,128]{1,0:T(8,128)S(1)}, f32[256,128]{1,0:T(8,128)S(1)}, u32[]{:S(2)}, u32[]{:S(2)}) collective-permute-start(f32[256,128]{1,0:T(8,128)S(1)} %bitcast.356), channel_id=1, source_target_pairs={{32,0},{48,16},{64,32},{80,48},{96,64},{112,80},{128,96},{144,112}... | collective-permute-start | bytes 393224 | tf_op jit(solution)/shard_map/ppermute | solution.py:16
  413.6 7.4 collective-permute-start.14
  414.9 11.4 %collective-permute-start.15 = (f32[256,128]{1,0:T(8,128)S(1)}, f32[256,128]{1,0:T(8,128)S(1)}, u32[]{:S(2)}, u32[]{:S(2)}) collective-permute-start(f32[256,128]{1,0:T(8,128)S(1)} %bitcast.354), channel_id=1, source_target_pairs={{64,0},{80,16},{96,32},{112,48},{128,64},{144,80},{160,96},{176,11... | collective-permute-start | bytes 393224 | tf_op jit(solution)/shard_map/ppermute | solution.py:16
  417.4 9.0 copy-start.2
  429.7 291.3 %reduce-scatter.20.cloned.1.call-start = ((), (), s32[]{:S(2)}) async-start(), calls=%async_computation.14 | async-start | bytes 1462272
  434.5 353.8 %reduce-scatter.18.cloned.1.call-start = ((), (), s32[]{:S(2)}) async-start(), calls=%async_computation.13 | async-start | bytes 1462272
  439.2 418.2 %reduce-scatter.16.cloned.1.call-start = ((), (), s32[]{:S(2)}) async-start(), calls=%async_computation.12 | async-start | bytes 2924544
  446.4 480.4 %reduce-scatter.22.cloned.1.call-start = ((), (), s32[]{:S(2)}) async-start(), calls=%async_computation.15 | async-start | bytes 2924544
Sparse Core Ops, SparseCore 0:
  9.8 37.7 all-gather.8
  50.2 89.5 all-gather.6
  141.6 35.5 all-gather.10
  179.7 88.5 all-gather.14
  269.9 34.5 all-gather.16
  306.2 35.3 all-gather.12
  429.8 223.5 reduce-scatter.13
  656.5 64.4 reduce-scatter.19
  724.1 64.1 reduce-scatter.17
  791.2 66.1 reduce-scatter.15
  860.5 66.1 reduce-scatter.21
where the time goes:
time: 935 us; the launch traced here: 933 us
  waiting for transfers between devices  793 us (85%)
  starting transfers between devices  37.1 us (4%)
  matrix products  35.7 us (4%)
  local copies, waits for them, and re-layouts  31.4 us (3%)
  other arithmetic  22.1 us (2%)
  between operations  14.4 us (2%)
    unnamed x15, waiting for transfers between devices  275 us
    reduce_scatter x1, waiting for transfers between devices, shards(): lax.psum_scatter(token_term, 'tp', scatter_dimension=1, tiled=True)  201 us
    all_gather x1, waiting for transfers between devices, shards(): lax.all_gather(tokens, 'tp', axis=1, tiled=True)  92.1 us
    all_gather x1, waiting for transfers between devices, shards(): lax.all_gather(cotangent, 'tp', axis=1, tiled=True)  87.6 us
    ppermute x16, starting transfers between devices, from_behind(): return lax.ppermute(block, axis, route)  36.6 us
    all_gather x1, waiting for transfers between devices, shards(): lax.all_gather(w_out, 'seq', axis=1, tiled=True)  36.3 us
    all_gather x1, waiting for transfers between devices, shards(): lax.all_gather(w_key, 'seq', axis=0, tiled=True)  35 us
    all_gather x1, waiting for transfers between devices, shards(): lax.all_gather(w_value, 'seq', axis=0, tiled=True)  33.5 us
  transfers between devices with their start and end apart: 27, of which 15 were waited for; matrix products, arithmetic and copies ran while one was open for 8% of the time, Pallas kernels for 0%

commit v1 on v0

--- a/solution.py
+++ b/solution.py
@@ -8,6 +8,18 @@
 HD = 128
 WIN = 1024
 ATTN_SCALAR = 168
+
+
+def _name_roads(mine, axis_id, dimension_no):
+    return jnp.concatenate(
+        lax.all_to_all(
+            jnp.stack([mine for _ in range(lax.axis_size(axis_id))]),
+            axis_name=axis_id,
+            split_axis=0,
+            concat_axis=0,
+        ),
+        axis=dimension_no,
+    )
 
 
 def from_behind(block, axis, distance):
@@ -101,7 +113,7 @@
     reach = WIN // tok_rows
     full_tokens, full_cot = (
         lax.all_gather(tokens, "tp", axis=1, tiled=True),
-        lax.all_gather(cotangent, "tp", axis=1, tiled=True),
+        _name_roads(cotangent, "tp", 1),
     )
     query_full, key_full, value_full = (
         lax.all_gather(w_query, "seq", axis=0, tiled=True),

time: 935 us -> 855 us (0.914)
  waiting for transfers between devices: 793 us -> 696 us
  starting transfers between devices: 37.1 us -> 48.4 us
    all_gather x1 -> x0, waiting for transfers between devices: 87.6 us -> none  [shards(): lax.all_gather(cotangent, 'tp', axis=1, tiled=True)]
    all_gather x1, waiting for transfers between devices: 35 us -> 22.3 us  [shards(): lax.all_gather(w_key, 'seq', axis=0, tiled=True)]
    all_to_all x0 -> x1, starting transfers between devices: none -> 11.3 us  [_name_roads(): lax.all_to_all(jnp.stack([mine for _ in range(lax.axis_size(axis_id))]),...]
    unnamed x15 -> x14, waiting for transfers between devices: 275 us -> 275 us
  transfers between devices with their start and end apart: 27 -> 27, of which waited for: 15 -> 14; matrix products, arithmetic and copies ran while one was open for 8% -> 9% of each run, Pallas kernels for 0% -> 0%
where the time goes in v1:
time: 855 us; the launch traced here: 853 us
  waiting for transfers between devices  696 us (81%)
  starting transfers between devices  48.4 us (6%)
  matrix products  37.2 us (4%)
  local copies, waits for them, and re-layouts  35.9 us (4%)
  other arithmetic  21.4 us (3%)
  between operations  14.7 us (2%)
    unnamed x14, waiting for transfers between devices  275 us
    reduce_scatter x1, waiting for transfers between devices, shards(): lax.psum_scatter(token_term, 'tp', scatter_dimension=1, tiled=True)  198 us
    all_gather x1, waiting for transfers between devices, shards(): lax.all_gather(tokens, 'tp', axis=1, tiled=True)  101 us
    ppermute x16, starting transfers between devices, from_behind(): return lax.ppermute(block, axis, route)  36.6 us
    all_gather x1, waiting for transfers between devices, shards(): lax.all_gather(w_out, 'seq', axis=1, tiled=True)  34.8 us
    all_gather x1, waiting for transfers between devices, shards(): lax.all_gather(w_value, 'seq', axis=0, tiled=True)  33.5 us
    all_gather x1, waiting for transfers between devices, shards(): lax.all_gather(w_key, 'seq', axis=0, tiled=True)  22.3 us
    all_gather x1, waiting for transfers between devices, shards(): lax.all_gather(w_query, 'seq', axis=0, tiled=True)  20.5 us
  transfers between devices with their start and end apart: 27, of which 14 were waited for; matrix products, arithmetic and copies ran while one was open for 9% of the time, Pallas kernels for 0%

profile of v1, /device:TPU:32, one launch (start us, length us, event | category | flops | bytes accessed | tf_op | source)
XLA Modules:
  0.0 853.4 jit_solution(15889752976756701104)
XLA Ops:
  10.0 2.7 stack.2
  12.7 11.3 %all-to-all-start = ((bf16[16,256,336]{1,2,0:T(8,128)(2,1)}), bf16[16,256,336]{1,2,0:T(8,128)(2,1)}, u32[]{:S(2)}, u32[]{:S(2)}) async-start(bf16[16,256,336]{1,2,0:T(8,128)(2,1)} %stack.2), calls=%async_computation | async-start | bytes 5505024 | tf_op jit(solution)/shard_map/all_to_all | solution.py:15
  25.4 22.3 %all-gather.8.cloned.1.call-done = bf16[5376,128]{1,0:T(8,128)(2,1)} async-done(((bf16[336,128]{1,0:T(8,128)(2,1)}), bf16[5376,128]{1,0:T(8,128)(2,1)}) %all-gather.8.cloned.1.call-update) | async-done | bytes 1376272 | tf_op jit(solution)/shard_map/all_gather | solution.py:120
  47.8 100.8 %all-gather.6.cloned.1.call-done = bf16[256,5376]{0,1:T(8,128)(2,1)} async-done(((bf16[256,336]{0,1:T(8,128)(2,1)}), bf16[256,5376]{0,1:T(8,128)(2,1)}) %all-gather.6.cloned.1.call-update) | async-done | bytes 2752528 | tf_op jit(solution)/shard_map/all_gather | solution.py:115
  148.6 3.2 convolution_convert_fusion.7
  151.8 5.5 collective-permute-start
  157.3 1.9 collective-permute-start.1
  159.2 3.1 collective-permute-start.2
  162.3 3.2 collective-permute-start.3
  165.5 20.5 %all-gather.10.cloned.1.call-done = bf16[5376,256]{1,0:T(8,128)(2,1)} async-done(((bf16[336,256]{1,0:T(8,128)(2,1)}), bf16[5376,256]{1,0:T(8,128)(2,1)}) %all-gather.10.cloned.1.call-update) | async-done | bytes 2752528 | tf_op jit(solution)/shard_map/all_gather | solution.py:119
  186.1 3.4 convolution_convert_fusion.5
  189.4 34.8 %all-gather.14.cloned.1.call-done = bf16[256,5376]{0,1:T(8,128)(2,1)} async-done(((bf16[256,336]{0,1:T(8,128)(2,1)}), bf16[256,5376]{0,1:T(8,128)(2,1)}) %all-gather.14.cloned.1.call-update) | async-done | bytes 2752528 | tf_op jit(solution)/shard_map/all_gather | solution.py:123
  224.3 3.5 convolution_convert_fusion.4
  227.8 33.5 %all-gather.12.cloned.1.call-done = bf16[5376,128]{1,0:T(8,128)(2,1)} async-done(((bf16[336,128]{1,0:T(8,128)(2,1)}), bf16[5376,128]{1,0:T(8,128)(2,1)}) %all-gather.12.cloned.1.call-update) | async-done | bytes 1376272 | tf_op jit(solution)/shard_map/all_gather | solution.py:121
  261.3 2.3 convolution_convert_fusion.6
  264.3 1.0 reshape.840
  265.3 1.6 reshape.813
  266.9 1.7 copy.87
  268.6 1.7 copy.98
  270.3 4.0 collective-permute-start.4
  275.1 2.0 collective-permute-start.5
  277.9 3.5 collective-permute-start.6
  281.4 3.0 collective-permute-start.7
  288.0 1.4 fusion.79
  289.9 1.8 convolution_bitcast_fusion.1
  293.6 1.5 fusion.11
  295.5 2.7 copy.100
  300.1 0.9 fusion.53
  301.1 0.9 fusion.51
  303.9 0.9 fusion.45
  304.8 0.9 fusion.43
  305.8 1.7 fusion.41
  307.5 1.3 collective-permute-start.12
  308.8 2.7 copy.89
  313.4 0.9 fusion.66
  319.0 1.7 fusion.54
  320.8 1.3 collective-permute-start.10
  322.0 1.3 collective-permute-start.11
  323.3 1.3 collective-permute-start.8
  324.6 1.5 collective-permute-start.9
  326.3 2.8 fusion.39
  329.1 1.3 collective-permute-start.13
  330.4 2.9 collective-permute-done.11
  333.4 1.3 collective-permute-start.14
  334.7 1.3 collective-permute-start.15
  336.0 1.1 fusion.74
  338.0 1.4 collective-permute-done.13
  339.4 1.4 collective-permute-done.14
  340.8 5.3 collective-permute-done.15
  346.1 3.3 convolution_add_fusion
  349.5 2.2 fusion.3
  351.7 2.5 copy.132
  354.3 2.2 fusion.2
  356.4 2.5 copy.130
  359.2 4.3 fusion.1
  363.5 4.7 copy.134
  368.2 2.6 fusion
  370.8 4.5 copy.128
  375.3 198.0 %reduce-scatter.14.cloned.1.call-done = f32[256,336]{0,1:T(8,128)} async-done(((f32[256,5376]{0,1:T(8,128)}), f32[256,336]{0,1:T(8,128)}) %reduce-scatter.14.cloned.1.call-update) | async-done | bytes 344080 | tf_op jit(solution)/shard_map/reduce_scatter | solution.py:166
  573.3 1.7 convert_element_type.114
  575.0 65.8 %reduce-scatter.20.cloned.1.call-done = bf16[336,128]{1,0:T(8,128)(2,1)} async-done(((bf16[5376,128]{1,0:T(8,128)(2,1)}), bf16[336,128]{1,0:T(8,128)(2,1)}) %reduce-scatter.20.cloned.1.call-update) | async-done | bytes 86032
  640.8 67.3 %reduce-scatter.18.cloned.1.call-done = bf16[336,128]{1,0:T(8,128)(2,1)} async-done(((bf16[5376,128]{1,0:T(8,128)(2,1)}), bf16[336,128]{1,0:T(8,128)(2,1)}) %reduce-scatter.18.cloned.1.call-update) | async-done | bytes 86032
  708.1 69.3 %reduce-scatter.22.cloned.1.call-done = bf16[336,256]{1,0:T(8,128)(2,1)} async-done(((bf16[5376,256]{1,0:T(8,128)(2,1)}), bf16[336,256]{1,0:T(8,128)(2,1)}) %reduce-scatter.22.cloned.1.call-update) | async-done | bytes 172048
  777.4 69.2 %reduce-scatter.16.cloned.1.call-done = bf16[336,256]{1,0:T(8,128)(2,1)} async-done(((bf16[5376,256]{1,0:T(8,128)(2,1)}), bf16[336,256]{1,0:T(8,128)(2,1)}) %reduce-scatter.16.cloned.1.call-update) | async-done | bytes 172048
  (104 shorter events, 24.5 us)
Async XLA Ops:
  7.2 40.6 %all-gather.8.cloned.1.call-start = ((), (), s32[]{:S(2)}) async-start(), calls=%async_computation.7 | async-start | bytes 1462272 | tf_op jit(solution)/shard_map/all_gather | solution.py:120
  7.9 140.7 %all-gather.6.cloned.1.call-start = ((), (), s32[]{:S(2)}) async-start(), calls=%async_computation.6 | async-start | bytes 2924544 | tf_op jit(solution)/shard_map/all_gather | solution.py:115
  8.6 177.4 %all-gather.10.cloned.1.call-start = ((), (), s32[]{:S(2)}) async-start(), calls=%async_computation.8 | async-start | bytes 2924544 | tf_op jit(solution)/shard_map/all_gather | solution.py:119
  9.4 214.9 %all-gather.14.cloned.1.call-start = ((), (), s32[]{:S(2)}) async-start(), calls=%async_computation.10 | async-start | bytes 2924544 | tf_op jit(solution)/shard_map/all_gather | solution.py:123
  12.7 12.0 %copy-start.10 = (s32[2,9]{1,0:T(2,128)S(1)}, s32[2,9]{1,0:T(2,128)}, u32[]{:S(2)}) copy-start(s32[2,9]{1,0:T(2,128)} %param.49) | copy-start | bytes 220
  12.7 176.8 %all-to-all-start = ((bf16[16,256,336]{1,2,0:T(8,128)(2,1)}), bf16[16,256,336]{1,2,0:T(8,128)(2,1)}, u32[]{:S(2)}, u32[]{:S(2)}) async-start(bf16[16,256,336]{1,2,0:T(8,128)(2,1)} %stack.2), calls=%async_computation | async-start | bytes 5505024 | tf_op jit(solution)/shard_map/all_to_all | solution.py:15
  24.0 237.3 %all-gather.12.cloned.1.call-start = ((), (), s32[]{:S(2)}) async-start(), calls=%async_computation.9 | async-start | bytes 1462272 | tf_op jit(solution)/shard_map/all_gather | solution.py:121
  24.6 548.7 %reduce-scatter.14.cloned.1.call-start = ((), (), s32[]{:S(2)}) async-start(), calls=%async_computation.11 | async-start | bytes 5849088 | tf_op jit(solution)/shard_map/reduce_scatter | solution.py:166
  148.6 37.5 %copy-start = (bf16[256,5376]{0,1:T(8,128)(2,1)S(1)}, bf16[256,5376]{0,1:T(8,128)(2,1)}, u32[]{:S(2)}) copy-start(bf16[256,5376]{0,1:T(8,128)(2,1)} %all-gather.6.cloned.1.call-done) | copy-start | bytes 8257540
  151.8 123.3 %collective-permute-start = (bf16[256,128]{1,0:T(8,128)(2,1)S(1)}, bf16[256,128]{1,0:T(8,128)(2,1)}, u32[]{:S(2)}, u32[]{:S(2)}) collective-permute-start(bf16[256,128]{1,0:T(8,128)(2,1)S(1)} %convolution_convert_fusion.7), channel_id=1, source_target_pairs={{0,64},{16,80},{32,96},{48,112},{64,128},{80,144},{96,160},{112,17... | collective-permute-start | bytes 196616 | tf_op jit(solution)/shard_map/ppermute | solution.py:28
  157.3 120.6 %collective-permute-start.1 = (bf16[256,128]{1,0:T(8,128)(2,1)S(1)}, bf16[256,128]{1,0:T(8,128)(2,1)}, u32[]{:S(2)}, u32[]{:S(2)}) collective-permute-start(bf16[256,128]{1,0:T(8,128)(2,1)S(1)} %convolution_convert_fusion.7), channel_id=1, source_target_pairs={{0,48},{16,64},{32,80},{48,96},{64,112},{80,128},{96,144},{112,160... | collective-permute-start | bytes 196616 | tf_op jit(solution)/shard_map/ppermute | solution.py:28
  159.2 122.2 %collective-permute-start.2 = (bf16[256,128]{1,0:T(8,128)(2,1)S(1)}, bf16[256,128]{1,0:T(8,128)(2,1)}, u32[]{:S(2)}, u32[]{:S(2)}) collective-permute-start(bf16[256,128]{1,0:T(8,128)(2,1)S(1)} %convolution_convert_fusion.7), channel_id=1, source_target_pairs={{0,32},{16,48},{32,64},{48,80},{64,96},{80,112},{96,128},{112,144}... | collective-permute-start | bytes 196616 | tf_op jit(solution)/shard_map/ppermute | solution.py:28
  162.3 122.1 %collective-permute-start.3 = (bf16[256,128]{1,0:T(8,128)(2,1)S(1)}, bf16[256,128]{1,0:T(8,128)(2,1)}, u32[]{:S(2)}, u32[]{:S(2)}) collective-permute-start(bf16[256,128]{1,0:T(8,128)(2,1)S(1)} %convolution_convert_fusion.7), channel_id=1, source_target_pairs={{0,16},{16,32},{32,48},{48,64},{64,80},{80,96},{96,112},{112,128},... | collective-permute-start | bytes 196616 | tf_op jit(solution)/shard_map/ppermute | solution.py:28
  227.8 35.8 %copy-start.4 = (bf16[256,256]{1,0:T(8,128)(2,1)}, bf16[256,256]{1,0:T(8,128)(2,1)S(1)}, u32[]{:S(2)}) copy-start(bf16[256,256]{1,0:T(8,128)(2,1)S(1)} %convolution_convert_fusion.4) | copy-start | bytes 393220
  270.3 21.4 %collective-permute-start.4 = (bf16[256,128]{1,0:T(8,128)(2,1)S(1)}, bf16[256,128]{1,0:T(8,128)(2,1)S(1)}, u32[]{:S(2)}, u32[]{:S(2)}) collective-permute-start(bf16[256,128]{1,0:T(8,128)(2,1)S(1)} %convolution_convert_fusion.6), channel_id=1, source_target_pairs={{0,64},{16,80},{32,96},{48,112},{64,128},{80,144},{96,160},{112,17... | collective-permute-start | bytes 196616 | tf_op jit(solution)/shard_map/ppermute | solution.py:28
  275.1 16.6 %collective-permute-start.5 = (bf16[256,128]{1,0:T(8,128)(2,1)S(1)}, bf16[256,128]{1,0:T(8,128)(2,1)S(1)}, u32[]{:S(2)}, u32[]{:S(2)}) collective-permute-start(bf16[256,128]{1,0:T(8,128)(2,1)S(1)} %convolution_convert_fusion.6), channel_id=1, source_target_pairs={{0,48},{16,64},{32,80},{48,96},{64,112},{80,128},{96,144},{112,160... | collective-permute-start | bytes 196616 | tf_op jit(solution)/shard_map/ppermute | solution.py:28
  277.9 13.8 %collective-permute-start.6 = (bf16[256,128]{1,0:T(8,128)(2,1)S(1)}, bf16[256,128]{1,0:T(8,128)(2,1)S(1)}, u32[]{:S(2)}, u32[]{:S(2)}) collective-permute-start(bf16[256,128]{1,0:T(8,128)(2,1)S(1)} %convolution_convert_fusion.6), channel_id=1, source_target_pairs={{0,32},{16,48},{32,64},{48,80},{64,96},{80,112},{96,128},{112,144}... | collective-permute-start | bytes 196616 | tf_op jit(solution)/shard_map/ppermute | solution.py:28
  281.4 10.3 %collective-permute-start.7 = (bf16[256,128]{1,0:T(8,128)(2,1)S(1)}, bf16[256,128]{1,0:T(8,128)(2,1)S(1)}, u32[]{:S(2)}, u32[]{:S(2)}) collective-permute-start(bf16[256,128]{1,0:T(8,128)(2,1)S(1)} %convolution_convert_fusion.6), channel_id=1, source_target_pairs={{0,16},{16,32},{32,48},{48,64},{64,80},{80,96},{96,112},{112,128},... | collective-permute-start | bytes 196616 | tf_op jit(solution)/shard_map/ppermute | solution.py:28
  288.0 1.9 copy-start.6
  289.9 2.0 copy-start.5
  292.7 0.9 copy-start.3
  307.5 30.5 %collective-permute-start.12 = (f32[256,128]{1,0:T(8,128)}, f32[256,128]{1,0:T(8,128)S(1)}, u32[]{:S(2)}, u32[]{:S(2)}) collective-permute-start(f32[256,128]{1,0:T(8,128)} %bitcast.75), channel_id=1, source_target_pairs={{16,0},{32,16},{48,32},{64,48},{80,64},{96,80},{112,96},{128,112},... | collective-permute-start | bytes 393224 | tf_op jit(solution)/shard_map/ppermute | solution.py:28
  320.8 8.4 collective-permute-start.10
  322.0 11.3 %collective-permute-start.11 = (f32[256,128]{1,0:T(8,128)}, f32[256,128]{1,0:T(8,128)}, u32[]{:S(2)}, u32[]{:S(2)}) collective-permute-start(f32[256,128]{1,0:T(8,128)} %bitcast.59), channel_id=1, source_target_pairs={{64,0},{80,16},{96,32},{112,48},{128,64},{144,80},{160,96},{176,11... | collective-permute-start | bytes 393224 | tf_op jit(solution)/shard_map/ppermute | solution.py:28
  323.3 11.3 %collective-permute-start.8 = (f32[256,128]{1,0:T(8,128)}, f32[256,128]{1,0:T(8,128)}, u32[]{:S(2)}, u32[]{:S(2)}) collective-permute-start(f32[256,128]{1,0:T(8,128)} %bitcast.56), channel_id=1, source_target_pairs={{16,0},{32,16},{48,32},{64,48},{80,64},{96,80},{112,96},{128,112},... | collective-permute-start | bytes 393224 | tf_op jit(solution)/shard_map/ppermute | solution.py:28
  324.6 11.3 %collective-permute-start.9 = (f32[256,128]{1,0:T(8,128)}, f32[256,128]{1,0:T(8,128)}, u32[]{:S(2)}, u32[]{:S(2)}) collective-permute-start(f32[256,128]{1,0:T(8,128)} %bitcast.57), channel_id=1, source_target_pairs={{32,0},{48,16},{64,32},{80,48},{96,64},{112,80},{128,96},{144,112}... | collective-permute-start | bytes 393224 | tf_op jit(solution)/shard_map/ppermute | solution.py:28
  326.3 2.9 copy-start.9
  326.3 7.1 copy-start.8
  326.3 8.4 copy-start.7
  326.3 10.8 %copy-start.1 = (bf16[5376,128]{1,0:T(8,128)(2,1)S(1)}, bf16[5376,128]{1,0:T(8,128)(2,1)}, u32[]{:S(2)}) copy-start(bf16[5376,128]{1,0:T(8,128)(2,1)} %all-gather.8.cloned.1.call-done) | copy-start | bytes 4128772
  329.1 10.2 %collective-permute-start.13 = (f32[256,128]{1,0:T(8,128)S(1)}, f32[256,128]{1,0:T(8,128)S(1)}, u32[]{:S(2)}, u32[]{:S(2)}) collective-permute-start(f32[256,128]{1,0:T(8,128)S(1)} %bitcast.359), channel_id=1, source_target_pairs={{32,0},{48,16},{64,32},{80,48},{96,64},{112,80},{128,96},{144,112}... | collective-permute-start | bytes 393224 | tf_op jit(solution)/shard_map/ppermute | solution.py:28
  333.4 7.4 collective-permute-start.14
  334.7 11.4 %collective-permute-start.15 = (f32[256,128]{1,0:T(8,128)S(1)}, f32[256,128]{1,0:T(8,128)S(1)}, u32[]{:S(2)}, u32[]{:S(2)}) collective-permute-start(f32[256,128]{1,0:T(8,128)S(1)} %bitcast.357), channel_id=1, source_target_pairs={{64,0},{80,16},{96,32},{112,48},{128,64},{144,80},{160,96},{176,11... | collective-permute-start | bytes 393224 | tf_op jit(solution)/shard_map/ppermute | solution.py:28
  337.1 9.0 %copy-start.2 = (bf16[5376,128]{1,0:T(8,128)(2,1)S(1)}, bf16[5376,128]{1,0:T(8,128)(2,1)}, u32[]{:S(2)}) copy-start(bf16[5376,128]{1,0:T(8,128)(2,1)} %all-gather.12.cloned.1.call-done) | copy-start | bytes 4128772
  349.4 291.4 %reduce-scatter.20.cloned.1.call-start = ((), (), s32[]{:S(2)}) async-start(), calls=%async_computation.14 | async-start | bytes 1462272
  354.2 353.9 %reduce-scatter.18.cloned.1.call-start = ((), (), s32[]{:S(2)}) async-start(), calls=%async_computation.13 | async-start | bytes 1462272
  359.0 418.4 %reduce-scatter.22.cloned.1.call-start = ((), (), s32[]{:S(2)}) async-start(), calls=%async_computation.15 | async-start | bytes 2924544
  368.1 478.4 %reduce-scatter.16.cloned.1.call-start = ((), (), s32[]{:S(2)}) async-start(), calls=%async_computation.12 | async-start | bytes 2924544
Sparse Core Ops, SparseCore 0:
  9.8 37.8 all-gather.7
  50.3 98.1 all-gather.5
  150.4 35.6 all-gather.9
  187.8 36.4 all-gather.13
  226.0 35.3 all-gather.11
  349.6 223.7 reduce-scatter.13
  576.4 64.3 reduce-scatter.19
  643.9 64.1 reduce-scatter.17
  711.2 66.1 reduce-scatter.21
  780.4 66.1 reduce-scatter.15
